TPU v7x, 128 devices: a whole 4x4x4 slice. The times are simulated.
128 devices in a mesh: gy: 16 (over y_hi, z, core), gz: 8 (over x, y_lo).
Axes of the slice: x: 4, y: 4 (y_hi: 2, y_lo: 2; y = y_hi * 2 + y_lo), z: 4, core: 2. Of those that a mesh axis runs over, the one named last changes fastest.
Arguments:
- field_in: bfloat16 [64, 256, 128, 256], P(None, 'gy', 'gz'), may hold values from -42 to 42
- spectral_weight: bfloat16 [32, 32, 32, 64, 128], P('gz', 'gy'), may hold values from -1.5258789e-05 to 1.5258789e-05
- point_weight: bfloat16 [64, 64], replicated, may hold values from -0.75 to 0.75
- point_bias: float32 [64], replicated, may hold values from -3 to 3
- out_weight: bfloat16 [64, 3], replicated, may hold values from -0.75 to 0.75
- out_bias: float32 [3], replicated, may hold values from -4 to 4
Outputs:
- loss_value: float32 [], replicated
- grad_spectral: float32 [32, 32, 32, 64, 128], P('gz', 'gy')
- grad_point: float32 [64, 64], replicated
- grad_point_bias: float32 [64], replicated
- grad_out: float32 [64, 3], replicated
- grad_out_bias: float32 [3], replicated
All inputs are finite; a program needn't handle non-finite values.
Results may differ from a plain program's by a relative error of at most 0.01.
Values may be sent and summed in bfloat16 or wider, within the bound.
A program may use at most 192 MiB of HBM per device.

v0:
```python
import math
import jax
import jax.numpy as jnp
from jax import lax
from jax.sharding import PartitionSpec as P

NX = 256
NY = 256
NZ = 128
MX = 32
MY = 32
MZ = 32


def with_halo(block, sides, width):
    for axis, dim in sides:
        count = lax.axis_size(axis)
        forward = [(i, i + 1) for i in range(count - 1)]
        backward = [(target, source) for source, target in forward]
        low = lax.ppermute(
            lax.slice_in_dim(block, block.shape[dim] - width, None, axis=dim), axis, forward
        )
        high = lax.ppermute(lax.slice_in_dim(block, 0, width, axis=dim), axis, backward)
        block = jnp.concatenate([low, block, high], axis=dim)
    return block


def frequencies(mode_count, mode_total):
    mode_index = jnp.arange(mode_count, dtype=jnp.int32)
    return jnp.where(mode_index < mode_total // 2, mode_index, mode_index - mode_total)


def twiddle(positions, wave_numbers, length):
    product = positions[:, None] * wave_numbers[None, :] % length
    phases = product.astype(jnp.float32) * (2.0 * math.pi / length)
    return (jnp.cos(phases).astype(jnp.bfloat16), jnp.sin(phases).astype(jnp.bfloat16))


def rotate(with_cos, with_sin, forward):
    half_width = with_cos.shape[-1] // 2
    cos_real, cos_imag = (with_cos[..., :half_width], with_cos[..., half_width:])
    sin_real, sin_imag = (with_sin[..., :half_width], with_sin[..., half_width:])
    if forward:
        return jnp.concatenate([cos_real + sin_imag, cos_imag - sin_real], axis=-1)
    return jnp.concatenate([cos_real - sin_imag, cos_imag + sin_real], axis=-1)


def x_tables(length, mode_total):
    cos_part, sin_part = twiddle(
        jnp.arange(length, dtype=jnp.int32), frequencies(mode_total, mode_total), length
    )
    forward_table = jnp.stack([cos_part, -sin_part], axis=1)
    inverse_table = jnp.stack([cos_part.T, -sin_part.T], axis=0)
    return (forward_table, inverse_table)


def cell_loss(field_b, slope_x, slope_y, slope_z):
    current_x = slope_y[2] - slope_z[1]
    current_y = slope_z[0] - slope_x[2]
    current_z = slope_x[1] - slope_y[0]
    force_x = current_y * field_b[2] - current_z * field_b[1]
    force_y = current_z * field_b[0] - current_x * field_b[2]
    force_z = current_x * field_b[1] - current_y * field_b[0]
    spread = slope_x[0] + slope_y[1] + slope_z[2]
    strength = field_b[0] * field_b[0] + field_b[1] * field_b[1] + field_b[2] * field_b[2] + 1.0
    return (force_x * force_x + force_y * force_y + force_z * force_z) / strength + spread * spread


def gelu_slope(pre_act):
    normal_cdf = 0.5 * (1.0 + lax.erf(pre_act * (1.0 / math.sqrt(2.0))))
    density = jnp.exp(-0.5 * pre_act * pre_act) * (1.0 / math.sqrt(2.0 * math.pi))
    return normal_cdf + pre_act * density


def to_modes(grid_field, factor, y_cells, z_cells, forward_table):
    channels, local_rows, local_depth = (
        grid_field.shape[0],
        grid_field.shape[1],
        grid_field.shape[2],
    )
    products = jnp.einsum(
        "cyzx,xpk->yzkpc", grid_field, forward_table, preferred_element_type=jnp.float32
    )
    x_modes = products.reshape(local_rows, local_depth, MX, 2 * channels).astype(jnp.bfloat16)
    y_cos, y_sin = twiddle(
        y_cells, frequencies(MY // lax.axis_size("gy") * lax.axis_size("gy"), MY), NY
    )
    with_cos = jnp.einsum("yzkc,yj->jzkc", x_modes, y_cos, preferred_element_type=jnp.float32)
    with_sin = jnp.einsum("yzkc,yj->jzkc", x_modes, y_sin, preferred_element_type=jnp.float32)
    y_modes = lax.psum_scatter(
        rotate(with_cos, with_sin, True), "gy", scatter_dimension=0, tiled=True
    ).astype(jnp.bfloat16)
    z_cos, z_sin = twiddle(
        z_cells, frequencies(MZ // lax.axis_size("gz") * lax.axis_size("gz"), MZ), NZ
    )
    with_cos = jnp.einsum("bzkc,zj->jbkc", y_modes, z_cos, preferred_element_type=jnp.float32)
    with_sin = jnp.einsum("bzkc,zj->jbkc", y_modes, z_sin, preferred_element_type=jnp.float32)
    summed = lax.psum_scatter(
        rotate(with_cos, with_sin, True), "gz", scatter_dimension=0, tiled=True
    )
    return (summed * factor).astype(jnp.bfloat16)


def from_modes(modes_out, y_cells, z_cells):
    portion = lax.all_gather(modes_out, "gz", axis=0, tiled=True)
    z_cos, z_sin = twiddle(z_cells, frequencies(portion.shape[0], MZ), NZ)
    with_cos = jnp.einsum("jbkc,zj->bzkc", portion, z_cos, preferred_element_type=jnp.float32)
    with_sin = jnp.einsum("jbkc,zj->bzkc", portion, z_sin, preferred_element_type=jnp.float32)
    z_back = rotate(with_cos, with_sin, False).astype(jnp.bfloat16)
    portion = lax.all_gather(z_back, "gy", axis=0, tiled=True)
    y_cos, y_sin = twiddle(y_cells, frequencies(portion.shape[0], MY), NY)
    with_cos = jnp.einsum("jzkc,yj->yzkc", portion, y_cos, preferred_element_type=jnp.float32)
    with_sin = jnp.einsum("jzkc,yj->yzkc", portion, y_sin, preferred_element_type=jnp.float32)
    return rotate(with_cos, with_sin, False).astype(jnp.bfloat16)


def mix_modes(modes_in, spectral_weight):
    channels = spectral_weight.shape[-2]
    with_real = jnp.einsum(
        "abki,abkio->abko",
        modes_in[..., :channels],
        spectral_weight,
        preferred_element_type=jnp.float32,
    )
    with_imag = jnp.einsum(
        "abki,abkio->abko",
        modes_in[..., channels:],
        spectral_weight,
        preferred_element_type=jnp.float32,
    )
    return jnp.concatenate(
        [
            with_real[..., :channels] - with_imag[..., channels:],
            with_real[..., channels:] + with_imag[..., :channels],
        ],
        axis=-1,
    ).astype(jnp.bfloat16)


def weight_grad(modes_in, grad_modes):
    channels = modes_in.shape[-1] // 2
    with_real = jnp.einsum(
        "abki,abko->abkio", modes_in[..., :channels], grad_modes, preferred_element_type=jnp.float32
    )
    with_imag = jnp.einsum(
        "abki,abko->abkio", modes_in[..., channels:], grad_modes, preferred_element_type=jnp.float32
    )
    return jnp.concatenate(
        [
            with_real[..., :channels] + with_imag[..., channels:],
            with_real[..., channels:] - with_imag[..., :channels],
        ],
        axis=-1,
    )


def on_device(field_in, spectral_weight, point_weight, point_bias, out_weight, out_bias):
    channels, local_rows, local_depth, x_count = field_in.shape
    y_cells = lax.axis_index("gy") * local_rows + jnp.arange(local_rows, dtype=jnp.int32)
    z_cells = lax.axis_index("gz") * local_depth + jnp.arange(local_depth, dtype=jnp.int32)
    forward_table, inverse_table = x_tables(x_count, MX)
    modes_in = to_modes(
        field_in, math.sqrt(MX * MY * MZ / (NX * NY * NZ)), y_cells, z_cells, forward_table
    )
    modes_out = mix_modes(modes_in, spectral_weight)
    y_back = from_modes(modes_out, y_cells, z_cells)
    spectral = jnp.einsum(
        "yzkpc,pkx->cyzx",
        y_back.reshape(local_rows, local_depth, MX, 2, channels),
        inverse_table,
        preferred_element_type=jnp.float32,
    )
    pointwise = jnp.einsum(
        "cyzx,co->oyzx", field_in, point_weight, preferred_element_type=jnp.float32
    )
    pre_act = spectral + pointwise + point_bias[:, None, None, None]
    hidden = jax.nn.gelu(pre_act, approximate=False).astype(jnp.bfloat16)
    b_field = (
        jnp.einsum("cyzx,cb->byzx", hidden, out_weight, preferred_element_type=jnp.float32)
        + out_bias[:, None, None, None]
    )
    padded = with_halo(b_field, (("gy", 1), ("gz", 2)), 2)
    widened = padded[:, 1:-1, 1:-1]
    x_padded = jnp.pad(widened, ((0, 0), (0, 0), (0, 0), (1, 1)))
    slope_x = (x_padded[..., 2:] - x_padded[..., :-2]) * 0.5
    slope_y = (padded[:, 2:, 1:-1] - padded[:, :-2, 1:-1]) * 0.5
    slope_z = (padded[:, 1:-1, 2:] - padded[:, 1:-1, :-2]) * 0.5
    cell_terms, pullback = jax.vjp(cell_loss, widened, slope_x, slope_y, slope_z)
    y_wide = lax.axis_index("gy") * local_rows - 1 + jnp.arange(local_rows + 2, dtype=jnp.int32)
    z_wide = lax.axis_index("gz") * local_depth - 1 + jnp.arange(local_depth + 2, dtype=jnp.int32)
    inside = ((y_wide >= 0) & (y_wide < NY))[:, None] & ((z_wide >= 0) & (z_wide < NZ))[None, :]
    weight_map = jnp.broadcast_to(
        jnp.where(inside, 1.0, 0.0)[:, :, None] / (NX * NY * NZ), cell_terms.shape
    ).astype(jnp.float32)
    grad_wide, grad_x, grad_y, grad_z = pullback(weight_map)
    gx_inner = jnp.pad(grad_x[:, 1:-1, 1:-1], ((0, 0), (0, 0), (0, 0), (1, 1)))
    grad_b = grad_wide[:, 1:-1, 1:-1] + (gx_inner[..., :-2] - gx_inner[..., 2:]) * 0.5
    grad_b = grad_b + (grad_y[:, :-2, 1:-1] - grad_y[:, 2:, 1:-1]) * 0.5
    grad_b = grad_b + (grad_z[:, 1:-1, :-2] - grad_z[:, 1:-1, 2:]) * 0.5
    loss_local = jnp.sum(cell_terms[1:-1, 1:-1])
    weights_f = out_weight.astype(jnp.float32)
    grad_hidden = jnp.zeros_like(pre_act)
    for component in range(3):
        grad_hidden = (
            grad_hidden + weights_f[:, component][:, None, None, None] * grad_b[component][None]
        )
    grad_pre = (grad_hidden * gelu_slope(pre_act)).astype(jnp.bfloat16)
    out_part = jnp.einsum(
        "cyzx,byzx->cb",
        hidden,
        grad_b,
        preferred_element_type=jnp.float32,
        precision=lax.Precision.HIGHEST,
    )
    out_bias_part = jnp.sum(grad_b, axis=(1, 2, 3))
    point_part = jnp.einsum("iyzx,oyzx->io", field_in, grad_pre, preferred_element_type=jnp.float32)
    point_bias_part = jnp.sum(grad_pre.astype(jnp.float32), axis=(1, 2, 3))
    totals = lax.psum(
        (loss_local, point_part, point_bias_part, out_part, out_bias_part), ("gy", "gz")
    )
    grad_modes = to_modes(grad_pre, 1.0, y_cells, z_cells, forward_table)
    grad_spectral = weight_grad(modes_in, grad_modes)
    return (totals[0] / (NX * NY * NZ), grad_spectral, totals[1], totals[2], totals[3], totals[4])


def solution(mesh):
    return jax.shard_map(
        on_device,
        mesh=mesh,
        in_specs=(P(None, "gy", "gz", None), P("gz", "gy", None, None, None), P(), P(), P(), P()),
        out_specs=(P(), P("gz", "gy", None, None, None), P(), P(), P(), P()),
        check_vma=False,
    )
```

profile of v0, /device:TPU:1, one launch (start us, length us, event | category | flops | bytes accessed | tf_op | source)
XLA Modules:
  0.0 781.1 jit_solution(12357975820388527888)
XLA Ops:
  7.7 13.6 %convert_bitcast_fusion.1 = bf16[16,16,32,2,64]{4,2,1,0,3:T(8,128)(2,1)S(1)} fusion(bf16[64,16,16,256]{3,2,1,0:T(8,128)(2,1)} %param.6, bf16[256,1,32]{0,2,1:T(8,128)(2,1)S(1)} %fusion.88, bf16[256,1,32]{0,2,1:T(8,128)(2,1)S(1)} %cosine_convert_fusion), kind=kOutput, calls=%fused_computation.58 | convolution fusion | flops 537985024 | bytes 10518528 | tf_op jit(solution)/shard_map/cyzx,xpk->yzkpc/dot_general | solution.py:81
  21.2 6.8 copy.89
  28.0 6.8 reshape.338
  34.8 4.8 fusion.109
  39.6 4.7 fusion.114
  44.3 18.8 %slice_add_fusion.2 = (f32[32,16,32,64]{3,0,2,1:T(8,128)}, f32[32,16,32,64]{3,0,2,1:T(8,128)}) fusion(f32[32,16,32,128]{3,0,2,1:T(8,128)} %fusion.109, f32[32,16,32,128]{3,0,2,1:T(8,128)} %fusion.114), kind=kLoop, calls=%fused_computation.36 | loop fusion | flops 2097152 | bytes 25165824 | tf_op jit(solution)/shard_map/add | solution.py:44
  63.1 11.4 %pad_maximum_fusion = f32[32,16,32,128]{3,0,2,1:T(8,128)} fusion(f32[32,16,32,64]{3,0,2,1:T(8,128)} %get-tuple-element.63, f32[32,16,32,64]{3,0,2,1:T(8,128)} %get-tuple-element.62), kind=kLoop, calls=%fused_computation.37 | loop fusion | flops 2097152 | bytes 16777216 | tf_op jit(solution)/shard_map/concatenate | solution.py:44
  74.5 11.5 %copy.52 = f32[32,16,32,128]{3,2,1,0:T(8,128)} copy(f32[32,16,32,128]{3,0,2,1:T(8,128)} %pad_maximum_fusion) | data formatting | bytes 16777216 | tf_op jit(solution)/shard_map/concatenate | solution.py:44
  86.1 104.2 %reduce-scatter.5.cloned.1.call-done = f32[2,16,32,128]{3,2,1,0:T(8,128)} async-done(((f32[32,16,32,128]{3,2,1,0:T(8,128)}), f32[2,16,32,128]{3,2,1,0:T(8,128)}) %reduce-scatter.5.cloned.1.call-update) | async-done | bytes 524304 | tf_op jit(solution)/shard_map/reduce_scatter | solution.py:90
  194.9 34.7 %reduce-scatter.7.cloned.1.call-done = f32[4,2,32,128]{3,2,1,0:T(8,128)} async-done(((f32[32,2,32,128]{3,2,1,0:T(8,128)}), f32[4,2,32,128]{3,2,1,0:T(8,128)}) %reduce-scatter.7.cloned.1.call-update) | async-done | bytes 131088 | tf_op jit(solution)/shard_map/reduce_scatter | solution.py:98
  238.3 23.3 %all_gather.6 = bf16[32,2,32,128]{3,2,1,0:T(8,128)(2,1)S(1)} all-gather(bf16[4,2,32,128]{3,2,1,0:T(8,128)(2,1)S(1)} %pad_maximum_fusion.17), channel_id=1, replica_groups=mesh['gy'=16,'gz'=8] {'gz'}, dimensions={0}, use_global_device_ids=true | all-gather | bytes 589824 | tf_op jit(solution)/shard_map/all_gather | solution.py:105
  264.3 65.5 %all-gather.2.cloned.1.call-done = bf16[32,16,32,128]{3,2,1,0:T(8,128)(2,1)} async-done(((bf16[2,16,32,128]{3,2,1,0:T(8,128)(2,1)}), bf16[32,16,32,128]{3,2,1,0:T(8,128)(2,1)}) %all-gather.2.cloned.1.call-update) | async-done | bytes 4194320 | tf_op jit(solution)/shard_map/all_gather | solution.py:110
  329.8 4.9 fusion.29
  340.8 8.1 %fusion.27 = f32[256,16,16,64,1]{0,3,4,2,1:T(8,128)} fusion(bf16[16,16,32,2,64]{4,0,2,1,3:T(8,128)(2,1)S(1)} %pad_maximum_fusion.3, bf16[1,32,256]{2,1,0:T(8,128)(2,1)S(1)} %fusion.87, bf16[1,32,256]{2,1,0:T(8,128)(2,1)S(1)} %cosine_convert_fusion.1), kind=kOutput, calls=%fused_computation.53 | convolution fusion | flops 536936448 | bytes 18907136 | tf_op jit(solution)/shard_map/yzkpc,pkx->cyzx/dot_general | solution.py:167
  348.9 19.3 %fusion.16 = (u16[64,16,256]{2,0,1:T(8,128)(2,1)S(1)}, f32[64,16,16,256]{3,0,2,1:T(8,128)}) fusion(f32[64]{0:T(128)S(1)} %copy-done.9, bf16[64,16,16,256]{3,2,1,0:T(8,128)(2,1)} %param.6, bf16[64,64]{1,0:T(8,128)(2,1)S(1)} %copy-done, f32[256,16,16,64,1]{0,3,4,2,1:T(8,128)} %fusion.27), kind=kOutput, calls=%fused_computation.30 | convolution fusion | flops 574357504 | bytes 42475776 | tf_op jit(solution)/shard_map/cyzx,co->oyzx/dot_general | solution.py:173
  368.2 39.0 %fusion.2 = bf16[64,16,16,256]{3,0,2,1:T(8,128)(2,1)S(1)} fusion(f32[64,16,16,256]{3,0,2,1:T(8,128)} %get-tuple-element.123, u16[64,16,256]{2,0,1:T(8,128)(2,1)S(1)} %get-tuple-element.122), kind=kLoop, calls=%fused_computation.4 | loop fusion | flops 285212672 | bytes 25690112 | tf_op jit(solution)/shard_map/convert_element_type | solution.py:177
  428.9 4.9 add_multiply_fusion
  447.1 11.2 %convert_reduce_fusion = (f32[64]{0:T(128)S(1)}, bf16[64,16,16,256]{3,0,2,1:T(8,128)(2,1)S(1)}) fusion(f32[64,16,16,256]{3,0,2,1:T(8,128)S(1)} %bitcast.132, f32[16,16,256]{2,1,0:T(8,128)S(1)} %bitcast.135, f32[64]{0:T(128)S(1)} %get-tuple-element.120, f32[16,16,256]{2,1,0:T(8,128)S(1)} %bitcast.136, f32[64]{0:T(128)S(1)} %get-tuple-element.121, ...), kind=kLoop, calls=%fused_computation.15 | loop fusion | flops 71303104 | bytes 25953280 | tf_op jit(solution)/shard_map/reduce_sum | solution.py:217
  465.8 6.3 copy.91
  472.1 7.2 reshape.339
  479.3 4.6 fusion.106
  483.9 4.6 fusion.111
  488.6 18.5 %slice_add_fusion.1 = (f32[32,16,32,64]{3,0,2,1:T(8,128)}, f32[32,16,32,64]{3,0,2,1:T(8,128)}) fusion(f32[32,16,32,128]{3,0,2,1:T(8,128)} %fusion.106, f32[32,16,32,128]{3,0,2,1:T(8,128)} %fusion.111), kind=kLoop, calls=%fused_computation.34 | loop fusion | flops 2097152 | bytes 25165824 | tf_op jit(solution)/shard_map/add | solution.py:44
  507.1 11.2 %pad_maximum_fusion.1 = f32[32,16,32,128]{3,0,2,1:T(8,128)} fusion(f32[32,16,32,64]{3,0,2,1:T(8,128)} %get-tuple-element.61, f32[32,16,32,64]{3,0,2,1:T(8,128)} %get-tuple-element.60), kind=kLoop, calls=%fused_computation.38 | loop fusion | flops 2097152 | bytes 16777216 | tf_op jit(solution)/shard_map/concatenate | solution.py:44
  518.3 11.5 %copy.67 = f32[32,16,32,128]{3,2,1,0:T(8,128)} copy(f32[32,16,32,128]{3,0,2,1:T(8,128)} %pad_maximum_fusion.1) | data formatting | bytes 16777216 | tf_op jit(solution)/shard_map/concatenate | solution.py:44
  529.9 104.6 %reduce-scatter.9.cloned.1.call-done = f32[2,16,32,128]{3,2,1,0:T(8,128)} async-done(((f32[32,16,32,128]{3,2,1,0:T(8,128)}), f32[2,16,32,128]{3,2,1,0:T(8,128)}) %reduce-scatter.9.cloned.1.call-update) | async-done | bytes 524304 | tf_op jit(solution)/shard_map/reduce_scatter | solution.py:90
  639.8 9.0 %convolution_bitcast_fusion.2 = f32[64,3]{0,1:T(4,128)S(1)} fusion(bf16[64,16,16,256]{3,0,2,1:T(8,128)(2,1)} %copy-done.2, f32[3,16,16,256]{3,0,2,1:T(4,128)S(1)} %get-tuple-element.30), kind=kOutput, calls=%fused_computation.91 | convolution fusion | flops 150994944 | bytes 9175808 | tf_op jit(solution)/shard_map/cyzx,byzx->cb/dot_general | solution.py:208
  648.9 15.3 %fusion.45 = f32[64,64]{0,1:T(8,128)S(1)} fusion(bf16[64,16,16,256]{3,0,2,1:T(8,128)(2,1)} %copy-done.3, bf16[64,16,16,256]{3,2,1,0:T(8,128)(2,1)} %param.6), kind=kOutput, calls=%fused_computation.90 | convolution fusion | flops 536870912 | bytes 16793600 | tf_op jit(solution)/shard_map/iyzx,oyzx->io/dot_general | solution.py:216
  664.2 66.3 %all-reduce.20 = (f32[]{:T(128)}, f32[64,64]{0,1:T(8,128)S(1)}, f32[64]{0:T(128)}, f32[64,3]{0,1:T(4,128)}, f32[3]{0:T(128)}) all-reduce(f32[]{:T(128)} %slice_reduce_fusion, f32[64,64]{0,1:T(8,128)S(1)} %fusion.45, f32[64]{0:T(128)S(1)} %get-tuple-element.31, ...), channel_id=1, replica_groups=mesh['gy'=16,'gz'=8] {'gy','gz'}, use_global_device_ids=true, to_apply=%region_3.4 | all-reduce | flops 4356 | bytes 34848 | tf_op jit(solution)/shard_map/psum | solution.py:218
  732.8 8.4 %broadcast_multiply_fusion.1 = (f32[4,2,32,64,128]{4,3,2,1,0:T(8,128)}, f32[4,2,32,64,128]{4,3,2,1,0:T(8,128)}) fusion(f32[4,2,32,128]{3,2,1,0:T(8,128)S(1)} %convert_convert_fusion, f32[4,2,32,64]{3,2,1,0:T(8,128)S(1)} %copy-done.5, f32[4,2,32,64]{3,2,1,0:T(8,128)S(1)} %copy-done.6), kind=kLoop, calls=%fused_computation.56 | loop fusion | flops 4194304 | bytes 17039360 | tf_op jit(solution)/shard_map/abki,abko->abkio/dot_general | solution.py:142
  741.2 19.9 %slice_add_fusion = (f32[4,2,32,64,64]{4,3,2,1,0:T(8,128)}, f32[4,2,32,64,64]{4,3,2,1,0:T(8,128)}) fusion(f32[4,2,32,64,128]{4,3,2,1,0:T(8,128)} %get-tuple-element.114, f32[4,2,32,64,128]{4,3,2,1,0:T(8,128)} %get-tuple-element.113), kind=kLoop, calls=%fused_computation.32 | loop fusion | flops 2097152 | bytes 25165824 | tf_op jit(solution)/shard_map/add | solution.py:150
  761.1 12.1 %pad_maximum_fusion.2 = f32[4,2,32,64,128]{4,3,2,1,0:T(8,128)} fusion(f32[4,2,32,64,64]{4,3,2,1,0:T(8,128)} %get-tuple-element.59, f32[4,2,32,64,64]{4,3,2,1,0:T(8,128)} %get-tuple-element.58), kind=kLoop, calls=%fused_computation.39 | loop fusion | flops 2097152 | bytes 16777216 | tf_op jit(solution)/shard_map/concatenate | solution.py:148
  (108 shorter events, 71.7 us)
Async XLA Ops:
  7.2 341.8 %copy-start = (bf16[64,64]{1,0:T(8,128)(2,1)S(1)}, bf16[64,64]{1,0:T(8,128)(2,1)}, u32[]{:S(2)}) copy-start(bf16[64,64]{1,0:T(8,128)(2,1)} %param.8) | copy-start | bytes 24580
  7.2 183.1 %reduce-scatter.5.cloned.1.call-start = ((), (), s32[]{:S(2)}) async-start(), calls=%async_computation.4 | async-start | bytes 8912896 | tf_op jit(solution)/shard_map/reduce_scatter | solution.py:90
  86.0 143.6 %reduce-scatter.7.cloned.1.call-start = ((), (), s32[]{:S(2)}) async-start(), calls=%async_computation.5 | async-start | bytes 1179648 | tf_op jit(solution)/shard_map/reduce_scatter | solution.py:98
  194.9 135.0 %all-gather.2.cloned.1.call-start = ((), (), s32[]{:S(2)}) async-start(), calls=%async_computation.6 | async-start | bytes 4456448 | tf_op jit(solution)/shard_map/all_gather | solution.py:110
  263.8 370.7 %reduce-scatter.9.cloned.1.call-start = ((), (), s32[]{:S(2)}) async-start(), calls=%async_computation.7 | async-start | bytes 8912896 | tf_op jit(solution)/shard_map/reduce_scatter | solution.py:90
  329.8 4.9 copy-start.4
  340.8 8.1 %copy-start.9 = (f32[64]{0:T(128)S(1)}, f32[64]{0:T(128)}, u32[]{:S(2)}) copy-start(f32[64]{0:T(128)} %param.9) | copy-start | bytes 772
  368.2 39.1 %copy-start.7 = (bf16[64,3]{0,1:T(4,128)(2,1)S(1)}, bf16[64,3]{0,1:T(4,128)(2,1)}, u32[]{:S(2)}) copy-start(bf16[64,3]{0,1:T(4,128)(2,1)} %param.10) | copy-start | bytes 1156
  368.2 39.1 %copy-start.8 = (f32[3]{0:T(128)S(1)}, f32[3]{0:T(128)}, u32[]{:S(2)}) copy-start(f32[3]{0:T(128)} %param.11) | copy-start | bytes 40
  407.3 9.6 %copy-start.2 = (bf16[64,16,16,256]{3,0,2,1:T(8,128)(2,1)}, bf16[64,16,16,256]{3,0,2,1:T(8,128)(2,1)S(1)}, u32[]{:S(2)}) copy-start(bf16[64,16,16,256]{3,0,2,1:T(8,128)(2,1)S(1)} %fusion.2) | copy-start | bytes 25165828
  408.6 4.4 collective-permute-start
  410.5 6.3 collective-permute-start.1
  416.9 4.5 collective-permute-start.3
  419.1 6.7 collective-permute-start.2
  435.1 12.0 %slice-start = ((s8[16777216]{0:T(1024)(128)(4,1)}), s8[4194304]{0:T(1024)(128)(4,1)S(1)}, s32[]{:S(2)}) async-start(s8[16777216]{0:T(1024)(128)(4,1)} %bitcast.131), calls=%async_computation.9 | async-start | bytes 8388608
  436.2 10.8 %slice-start.1 = ((s8[16777216]{0:T(1024)(128)(4,1)}), s8[4194304]{0:T(1024)(128)(4,1)S(1)}, s32[]{:S(2)}) async-start(s8[16777216]{0:T(1024)(128)(4,1)} %bitcast.131), calls=%async_computation.10 | async-start | bytes 8388608
  440.7 6.4 slice-start.2
  442.2 4.8 slice-start.3
  458.3 3.4 copy-start.3
  529.9 202.0 %reduce-scatter.11.cloned.1.call-start = ((), (), s32[]{:S(2)}) async-start(), calls=%async_computation.8 | async-start | bytes 1179648 | tf_op jit(solution)/shard_map/reduce_scatter | solution.py:98
  648.8 83.9 %copy-start.5 = (f32[4,2,32,64]{3,2,1,0:T(8,128)S(1)}, f32[4,2,32,64]{3,2,1,0:T(8,128)}, u32[]{:S(2)}) copy-start(f32[4,2,32,64]{3,2,1,0:T(8,128)} %get-tuple-element.115) | copy-start | bytes 196612
  648.9 83.9 %copy-start.6 = (f32[4,2,32,64]{3,2,1,0:T(8,128)S(1)}, f32[4,2,32,64]{3,2,1,0:T(8,128)}, u32[]{:S(2)}) copy-start(f32[4,2,32,64]{3,2,1,0:T(8,128)} %get-tuple-element.116) | copy-start | bytes 196612
  761.1 12.1 %copy-start.1 = (bf16[64,64]{1,0:T(8,128)(2,1)S(1)}, bf16[64,64]{1,0:T(8,128)(2,1)}, u32[]{:S(2)}) copy-start(bf16[64,64]{1,0:T(8,128)(2,1)} %param.8) | copy-start | bytes 24580
Sparse Core Ops, SparseCore 0:
  86.1 104.1 reduce-scatter.4
  195.0 34.5 reduce-scatter.6
  263.9 65.8 all-gather.1
  530.0 104.5 reduce-scatter.8
  639.2 34.5 reduce-scatter.10
where the time goes:
time: 790 us; the launch traced here: 781 us
  waiting for transfers between devices  318 us (40%)
  other arithmetic  183 us (23%)
  matrix products  106 us (13%)
  blocking collectives  89.6 us (11%)
  local copies, waits for them, and re-layouts  59.1 us (7%)
  between operations  16.3 us (2%)
  starting transfers between devices  8.05 us (1%)
    reduce_scatter x2, waiting for transfers between devices, to_modes(): lax.psum_scatter(rotate(with_cos, with_sin, True), 'gy', scatter_dimensio...  209 us
    psum x1, blocking collectives, on_device(): lax.psum((loss_local, point_part, point_bias_part, out_part, out_bias_par...  66.3 us
    all_gather x1, waiting for transfers between devices, from_modes(): portion = lax.all_gather(z_back, 'gy', axis=0, tiled=True)  65.5 us
    convert_element_type x1, other arithmetic, on_device(): hidden = jax.nn.gelu(pre_act, approximate=False).astype(jnp.bfloat16)  39 us
    add x4, other arithmetic, rotate(): return jnp.concatenate([cos_real + sin_imag, cos_imag - sin_real], axis=-1)  38.6 us
    reduce_scatter x2, waiting for transfers between devices, to_modes(): lax.psum_scatter(rotate(with_cos, with_sin, True), 'gz', scatter_dimensio...  34.7 us
    convert_element_type x4, local copies, waits for them, and re-layouts, to_modes(): products.reshape(local_rows, local_depth, MX, 2 * channels)  27 us
    concatenate x4, local copies, waits for them, and re-layouts, rotate(): return jnp.concatenate([cos_real + sin_imag, cos_imag - sin_real], axis=-1)  26.2 us
  transfers between devices with their start and end apart: 9, of which 7 were waited for; matrix products, arithmetic and copies ran while one was open for 3% of the time, Pallas kernels for 0%

commit v1 on v0

--- a/solution.py
+++ b/solution.py
@@ -216,7 +216,10 @@
     point_part = jnp.einsum("iyzx,oyzx->io", field_in, grad_pre, preferred_element_type=jnp.float32)
     point_bias_part = jnp.sum(grad_pre.astype(jnp.float32), axis=(1, 2, 3))
     totals = lax.psum(
-        (loss_local, point_part, point_bias_part, out_part, out_bias_part), ("gy", "gz")
+        lax.psum(
+            (loss_local, point_part, point_bias_part, out_part, out_bias_part), axis_name="gy"
+        ),
+        "gz",
     )
     grad_modes = to_modes(grad_pre, 1.0, y_cells, z_cells, forward_table)
     grad_spectral = weight_grad(modes_in, grad_modes)

time: 790 us -> 827 us (1.047)
  the two profiles are of different devices: /device:TPU:1 before, /device:TPU:0 now
where the time goes in v1:
time: 827 us; the launch traced here: 818 us
  waiting for transfers between devices  314 us (38%)
  other arithmetic  183 us (22%)
  blocking collectives  132 us (16%)
  matrix products  106 us (13%)
  local copies, waits for them, and re-layouts  58.8 us (7%)
  between operations  16.3 us (2%)
    reduce_scatter x2, waiting for transfers between devices, to_modes(): lax.psum_scatter(rotate(with_cos, with_sin, True), 'gy', scatter_dimensio...  213 us
    psum x1, blocking collectives, on_device(): lax.psum((loss_local, point_part, point_bias_part, out_part, out_bias_par...  66.2 us
    all_gather x1, waiting for transfers between devices, from_modes(): portion = lax.all_gather(z_back, 'gy', axis=0, tiled=True)  53.8 us
    convert_element_type x1, other arithmetic, on_device(): hidden = jax.nn.gelu(pre_act, approximate=False).astype(jnp.bfloat16)  38.8 us
    reduce_scatter x2, waiting for transfers between devices, to_modes(): lax.psum_scatter(rotate(with_cos, with_sin, True), 'gz', scatter_dimensio...  38.8 us
    add x4, other arithmetic, rotate(): return jnp.concatenate([cos_real + sin_imag, cos_imag - sin_real], axis=-1)  38.7 us
    psum x1, blocking collectives, on_device(): lax.psum(lax.psum((loss_local, point_part, point_bias_part, out_part, out...  36.1 us
    all_gather x1, blocking collectives, from_modes(): portion = lax.all_gather(modes_out, 'gz', axis=0, tiled=True)  29.3 us
  transfers between devices with their start and end apart: 9, of which 7 were waited for; matrix products, arithmetic and copies ran while one was open for 3% of the time, Pallas kernels for 0%

profile of v1, /device:TPU:0, one launch (start us, length us, event | category | flops | bytes accessed | tf_op | source)
XLA Modules:
  0.0 817.7 jit_solution(8700051561253048024)
XLA Ops:
  7.7 13.6 %convert_bitcast_fusion.1 = bf16[16,16,32,2,64]{4,2,1,0,3:T(8,128)(2,1)S(1)} fusion(bf16[64,16,16,256]{3,2,1,0:T(8,128)(2,1)} %param.6, bf16[256,1,32]{0,2,1:T(8,128)(2,1)S(1)} %fusion.88, bf16[256,1,32]{0,2,1:T(8,128)(2,1)S(1)} %cosine_convert_fusion), kind=kOutput, calls=%fused_computation.58 | convolution fusion | flops 537985024 | bytes 10518528 | tf_op jit(solution)/shard_map/cyzx,xpk->yzkpc/dot_general | solution.py:81
  21.2 6.5 copy.89
  27.7 6.8 reshape.338
  34.5 4.8 fusion.109
  39.3 4.7 fusion.114
  44.0 18.8 %slice_add_fusion.2 = (f32[32,16,32,64]{3,0,2,1:T(8,128)}, f32[32,16,32,64]{3,0,2,1:T(8,128)}) fusion(f32[32,16,32,128]{3,0,2,1:T(8,128)} %fusion.109, f32[32,16,32,128]{3,0,2,1:T(8,128)} %fusion.114), kind=kLoop, calls=%fused_computation.36 | loop fusion | flops 2097152 | bytes 25165824 | tf_op jit(solution)/shard_map/add | solution.py:44
  62.8 11.4 %pad_maximum_fusion = f32[32,16,32,128]{3,0,2,1:T(8,128)} fusion(f32[32,16,32,64]{3,0,2,1:T(8,128)} %get-tuple-element.68, f32[32,16,32,64]{3,0,2,1:T(8,128)} %get-tuple-element.67), kind=kLoop, calls=%fused_computation.37 | loop fusion | flops 2097152 | bytes 16777216 | tf_op jit(solution)/shard_map/concatenate | solution.py:44
  74.2 11.5 %copy.52 = f32[32,16,32,128]{3,2,1,0:T(8,128)} copy(f32[32,16,32,128]{3,0,2,1:T(8,128)} %pad_maximum_fusion) | data formatting | bytes 16777216 | tf_op jit(solution)/shard_map/concatenate | solution.py:44
  85.8 105.0 %reduce-scatter.5.cloned.1.call-done = f32[2,16,32,128]{3,2,1,0:T(8,128)} async-done(((f32[32,16,32,128]{3,2,1,0:T(8,128)}), f32[2,16,32,128]{3,2,1,0:T(8,128)}) %reduce-scatter.5.cloned.1.call-update) | async-done | bytes 524304 | tf_op jit(solution)/shard_map/reduce_scatter | solution.py:90
  195.4 38.7 %reduce-scatter.7.cloned.1.call-done = f32[4,2,32,128]{3,2,1,0:T(8,128)} async-done(((f32[32,2,32,128]{3,2,1,0:T(8,128)}), f32[4,2,32,128]{3,2,1,0:T(8,128)}) %reduce-scatter.7.cloned.1.call-update) | async-done | bytes 131088 | tf_op jit(solution)/shard_map/reduce_scatter | solution.py:98
  242.8 29.3 %all_gather.6 = bf16[32,2,32,128]{3,2,1,0:T(8,128)(2,1)S(1)} all-gather(bf16[4,2,32,128]{3,2,1,0:T(8,128)(2,1)S(1)} %pad_maximum_fusion.17), channel_id=1, replica_groups=mesh['gy'=16,'gz'=8] {'gz'}, dimensions={0}, use_global_device_ids=true | all-gather | bytes 589824 | tf_op jit(solution)/shard_map/all_gather | solution.py:105
  274.9 53.8 %all-gather.2.cloned.1.call-done = bf16[32,16,32,128]{3,2,1,0:T(8,128)(2,1)} async-done(((bf16[2,16,32,128]{3,2,1,0:T(8,128)(2,1)}), bf16[32,16,32,128]{3,2,1,0:T(8,128)(2,1)}) %all-gather.2.cloned.1.call-update) | async-done | bytes 4194320 | tf_op jit(solution)/shard_map/all_gather | solution.py:110
  328.6 4.9 fusion.29
  339.5 8.1 fusion.27
  347.7 19.3 %fusion.16 = (u16[64,16,256]{2,0,1:T(8,128)(2,1)S(1)}, f32[64,16,16,256]{3,0,2,1:T(8,128)}) fusion(f32[64]{0:T(128)S(1)} %copy-done.9, bf16[64,16,16,256]{3,2,1,0:T(8,128)(2,1)} %param.6, bf16[64,64]{1,0:T(8,128)(2,1)S(1)} %copy-done, f32[256,16,16,64,1]{0,3,4,2,1:T(8,128)} %fusion.27), kind=kOutput, calls=%fused_computation.30 | convolution fusion | flops 574357504 | bytes 42475776 | tf_op jit(solution)/shard_map/cyzx,co->oyzx/dot_general | solution.py:173
  367.0 38.8 %fusion.2 = bf16[64,16,16,256]{3,0,2,1:T(8,128)(2,1)S(1)} fusion(f32[64,16,16,256]{3,0,2,1:T(8,128)} %get-tuple-element.128, u16[64,16,256]{2,0,1:T(8,128)(2,1)S(1)} %get-tuple-element.127), kind=kLoop, calls=%fused_computation.4 | loop fusion | flops 285212672 | bytes 25690112 | tf_op jit(solution)/shard_map/convert_element_type | solution.py:177
  417.9 4.7 collective-permute-done.2
  425.9 4.9 add_multiply_fusion
  444.1 11.2 %convert_reduce_fusion = (f32[64]{0:T(128)S(1)}, bf16[64,16,16,256]{3,0,2,1:T(8,128)(2,1)S(1)}) fusion(f32[64,16,16,256]{3,0,2,1:T(8,128)S(1)} %bitcast.132, f32[16,16,256]{2,1,0:T(8,128)S(1)} %bitcast.135, f32[64]{0:T(128)S(1)} %get-tuple-element.125, f32[16,16,256]{2,1,0:T(8,128)S(1)} %bitcast.136, f32[64]{0:T(128)S(1)} %get-tuple-element.126, ...), kind=kLoop, calls=%fused_computation.15 | loop fusion | flops 71303104 | bytes 25953280 | tf_op jit(solution)/shard_map/reduce_sum | solution.py:217
  462.8 6.3 copy.91
  469.1 7.2 reshape.339
  485.6 18.6 %slice_add_fusion.1 = (f32[32,16,32,64]{3,0,2,1:T(8,128)}, f32[32,16,32,64]{3,0,2,1:T(8,128)}) fusion(f32[32,16,32,128]{3,0,2,1:T(8,128)} %fusion.106, f32[32,16,32,128]{3,0,2,1:T(8,128)} %fusion.111), kind=kLoop, calls=%fused_computation.34 | loop fusion | flops 2097152 | bytes 25165824 | tf_op jit(solution)/shard_map/add | solution.py:44
  504.2 11.2 %pad_maximum_fusion.1 = f32[32,16,32,128]{3,0,2,1:T(8,128)} fusion(f32[32,16,32,64]{3,0,2,1:T(8,128)} %get-tuple-element.66, f32[32,16,32,64]{3,0,2,1:T(8,128)} %get-tuple-element.65), kind=kLoop, calls=%fused_computation.38 | loop fusion | flops 2097152 | bytes 16777216 | tf_op jit(solution)/shard_map/concatenate | solution.py:44
  515.4 11.5 %copy.67 = f32[32,16,32,128]{3,2,1,0:T(8,128)} copy(f32[32,16,32,128]{3,0,2,1:T(8,128)} %pad_maximum_fusion.1) | data formatting | bytes 16777216 | tf_op jit(solution)/shard_map/concatenate | solution.py:44
  527.0 108.1 %reduce-scatter.9.cloned.1.call-done = f32[2,16,32,128]{3,2,1,0:T(8,128)} async-done(((f32[32,16,32,128]{3,2,1,0:T(8,128)}), f32[2,16,32,128]{3,2,1,0:T(8,128)}) %reduce-scatter.9.cloned.1.call-update) | async-done | bytes 524304 | tf_op jit(solution)/shard_map/reduce_scatter | solution.py:90
  640.4 9.0 %convolution_bitcast_fusion.2 = f32[64,3]{0,1:T(4,128)S(1)} fusion(bf16[64,16,16,256]{3,0,2,1:T(8,128)(2,1)} %copy-done.2, f32[3,16,16,256]{3,0,2,1:T(4,128)S(1)} %get-tuple-element.35), kind=kOutput, calls=%fused_computation.91 | convolution fusion | flops 150994944 | bytes 9175808 | tf_op jit(solution)/shard_map/cyzx,byzx->cb/dot_general | solution.py:208
  649.4 15.3 %fusion.45 = f32[64,64]{0,1:T(8,128)S(1)} fusion(bf16[64,16,16,256]{3,0,2,1:T(8,128)(2,1)} %copy-done.3, bf16[64,16,16,256]{3,2,1,0:T(8,128)(2,1)} %param.6), kind=kOutput, calls=%fused_computation.90 | convolution fusion | flops 536870912 | bytes 16793600 | tf_op jit(solution)/shard_map/iyzx,oyzx->io/dot_general | solution.py:216
  664.8 66.2 %all-reduce.20 = (f32[]{:T(128)}, f32[64,64]{0,1:T(8,128)S(1)}, f32[64]{0:T(128)S(1)}, f32[64,3]{0,1:T(4,128)S(1)}, f32[3]{0:T(128)S(1)}) all-reduce(f32[]{:T(128)} %slice_reduce_fusion, f32[64,64]{0,1:T(8,128)S(1)} %fusion.45, f32[64]{0:T(128)S(1)} %get-tuple-element.36, ...), channel_id=1, replica_groups=mesh['gy'=16,'gz'=8] {'gy'}, use_global_device_ids=true, to_apply=%region_3.4 | all-reduce | flops 4356 | bytes 34848 | tf_op jit(solution)/shard_map/psum | solution.py:219
  731.0 36.1 %all-reduce.21 = (f32[]{:T(128)}, f32[64,64]{0,1:T(8,128)S(1)}, f32[64]{0:T(128)}, f32[64,3]{0,1:T(4,128)}, f32[3]{0:T(128)}) all-reduce(f32[]{:T(128)} %get-tuple-element.24, f32[64,64]{0,1:T(8,128)S(1)} %get-tuple-element.25, f32[64]{0:T(128)S(1)} %get-tuple-element.26, ...), channel_id=1, replica_groups=mesh['gy'=16,'gz'=8] {'gz'}, use_global_device_ids=true, to_apply=%region_4.5 | all-reduce | flops 4356 | bytes 34848 | tf_op jit(solution)/shard_map/psum | solution.py:218
  769.4 8.5 %broadcast_multiply_fusion.1 = (f32[4,2,32,64,128]{4,3,2,1,0:T(8,128)}, f32[4,2,32,64,128]{4,3,2,1,0:T(8,128)}) fusion(f32[4,2,32,128]{3,2,1,0:T(8,128)S(1)} %convert_convert_fusion, f32[4,2,32,64]{3,2,1,0:T(8,128)S(1)} %copy-done.5, f32[4,2,32,64]{3,2,1,0:T(8,128)S(1)} %copy-done.6), kind=kLoop, calls=%fused_computation.56 | loop fusion | flops 4194304 | bytes 17039360 | tf_op jit(solution)/shard_map/abki,abko->abkio/dot_general | solution.py:142
  777.8 19.8 %slice_add_fusion = (f32[4,2,32,64,64]{4,3,2,1,0:T(8,128)}, f32[4,2,32,64,64]{4,3,2,1,0:T(8,128)}) fusion(f32[4,2,32,64,128]{4,3,2,1,0:T(8,128)} %get-tuple-element.119, f32[4,2,32,64,128]{4,3,2,1,0:T(8,128)} %get-tuple-element.118), kind=kLoop, calls=%fused_computation.32 | loop fusion | flops 2097152 | bytes 25165824 | tf_op jit(solution)/shard_map/add | solution.py:150
  797.7 12.1 %pad_maximum_fusion.2 = f32[4,2,32,64,128]{4,3,2,1,0:T(8,128)} fusion(f32[4,2,32,64,64]{4,3,2,1,0:T(8,128)} %get-tuple-element.64, f32[4,2,32,64,64]{4,3,2,1,0:T(8,128)} %get-tuple-element.63), kind=kLoop, calls=%fused_computation.39 | loop fusion | flops 2097152 | bytes 16777216 | tf_op jit(solution)/shard_map/concatenate | solution.py:148
  (109 shorter events, 74.7 us)
Async XLA Ops:
  7.2 340.5 %copy-start = (bf16[64,64]{1,0:T(8,128)(2,1)S(1)}, bf16[64,64]{1,0:T(8,128)(2,1)}, u32[]{:S(2)}) copy-start(bf16[64,64]{1,0:T(8,128)(2,1)} %param.8) | copy-start | bytes 24580
  7.2 183.6 %reduce-scatter.5.cloned.1.call-start = ((), (), s32[]{:S(2)}) async-start(), calls=%async_computation.4 | async-start | bytes 8912896 | tf_op jit(solution)/shard_map/reduce_scatter | solution.py:90
  85.8 148.4 %reduce-scatter.7.cloned.1.call-start = ((), (), s32[]{:S(2)}) async-start(), calls=%async_computation.5 | async-start | bytes 1179648 | tf_op jit(solution)/shard_map/reduce_scatter | solution.py:98
  195.3 133.3 %all-gather.2.cloned.1.call-start = ((), (), s32[]{:S(2)}) async-start(), calls=%async_computation.6 | async-start | bytes 4456448 | tf_op jit(solution)/shard_map/all_gather | solution.py:110
  274.4 360.8 %reduce-scatter.9.cloned.1.call-start = ((), (), s32[]{:S(2)}) async-start(), calls=%async_computation.7 | async-start | bytes 8912896 | tf_op jit(solution)/shard_map/reduce_scatter | solution.py:90
  328.6 4.9 copy-start.4
  339.5 8.1 copy-start.9
  367.0 38.8 %copy-start.7 = (bf16[64,3]{0,1:T(4,128)(2,1)S(1)}, bf16[64,3]{0,1:T(4,128)(2,1)}, u32[]{:S(2)}) copy-start(bf16[64,3]{0,1:T(4,128)(2,1)} %param.10) | copy-start | bytes 1156
  367.0 38.8 %copy-start.8 = (f32[3]{0:T(128)S(1)}, f32[3]{0:T(128)}, u32[]{:S(2)}) copy-start(f32[3]{0:T(128)} %param.11) | copy-start | bytes 40
  405.8 6.8 copy-start.2
  407.1 3.5 collective-permute-start
  409.2 3.2 collective-permute-start.1
  412.6 5.3 collective-permute-start.3
  415.1 7.5 collective-permute-start.2
  432.1 12.0 %slice-start = ((s8[16777216]{0:T(1024)(128)(4,1)}), s8[4194304]{0:T(1024)(128)(4,1)S(1)}, s32[]{:S(2)}) async-start(s8[16777216]{0:T(1024)(128)(4,1)} %bitcast.131), calls=%async_computation.9 | async-start | bytes 8388608
  433.3 10.8 %slice-start.1 = ((s8[16777216]{0:T(1024)(128)(4,1)}), s8[4194304]{0:T(1024)(128)(4,1)S(1)}, s32[]{:S(2)}) async-start(s8[16777216]{0:T(1024)(128)(4,1)} %bitcast.131), calls=%async_computation.10 | async-start | bytes 8388608
  437.7 6.4 slice-start.2
  439.3 4.8 slice-start.3
  455.3 3.4 copy-start.3
  527.0 241.5 %reduce-scatter.11.cloned.1.call-start = ((), (), s32[]{:S(2)}) async-start(), calls=%async_computation.8 | async-start | bytes 1179648 | tf_op jit(solution)/shard_map/reduce_scatter | solution.py:98
  649.4 120.0 %copy-start.5 = (f32[4,2,32,64]{3,2,1,0:T(8,128)S(1)}, f32[4,2,32,64]{3,2,1,0:T(8,128)}, u32[]{:S(2)}) copy-start(f32[4,2,32,64]{3,2,1,0:T(8,128)} %get-tuple-element.120) | copy-start | bytes 196612
  649.4 120.0 %copy-start.6 = (f32[4,2,32,64]{3,2,1,0:T(8,128)S(1)}, f32[4,2,32,64]{3,2,1,0:T(8,128)}, u32[]{:S(2)}) copy-start(f32[4,2,32,64]{3,2,1,0:T(8,128)} %get-tuple-element.121) | copy-start | bytes 196612
  797.7 12.1 %copy-start.1 = (bf16[64,64]{1,0:T(8,128)(2,1)S(1)}, bf16[64,64]{1,0:T(8,128)(2,1)}, u32[]{:S(2)}) copy-start(bf16[64,64]{1,0:T(8,128)(2,1)} %param.8) | copy-start | bytes 24580
Sparse Core Ops, SparseCore 0:
  85.9 104.8 reduce-scatter.4
  195.5 38.6 reduce-scatter.6
  274.5 54.0 all-gather.1
  527.1 107.9 reduce-scatter.8
  639.8 38.5 reduce-scatter.10
